TPU v7x, 32 devices: a whole 2x2x4 slice. The times are simulated.
32 devices in a mesh: grp: 2 (over y), seq: 4 (over z), head: 2 (over x), sub: 2 (over core).
Axes of the slice: x: 2, y: 2, z: 4, core: 2. Of those that a mesh axis runs over, the one named last changes fastest.
Arguments:
- queries: bfloat16 [768, 5120], P(('grp', 'seq', 'head', 'sub')), parts along dimension 0, may hold values from -24 to 24
- keys: bfloat16 [768, 5120], P(('grp', 'seq', 'head', 'sub')), parts along dimension 0, may hold values from -24 to 24
- values: bfloat16 [768, 5120], P(('grp', 'seq', 'head', 'sub')), parts along dimension 0, may hold values from -6 to 6
- q_gain: float32 [5120], replicated, may hold values from 0.5 to 4
- k_gain: float32 [5120], replicated, may hold values from 0.5 to 4
Outputs:
- attended: bfloat16 [768, 5120], P(('grp', 'seq', 'head', 'sub')), parts along dimension 0
There are 2 independent parts, one for each index of `grp`. A program takes and returns all parts, laid end to end along the dimension named above; an argument that names none is the same for every part. Nothing has to cross between parts.
All inputs are finite; a program needn't handle non-finite values.
Results may differ from a plain program's by a relative error of at most 0.012.
The roundings to bfloat16 on the way count: a program that leaves them out, or rounds other values in their place, can miss the bound.
Values may be sent and summed in bfloat16 or wider, within the bound.
A program may use at most 64 MiB of HBM per device.

v0:
```python
import math

import jax
import jax.numpy as jnp
from jax import lax
from jax.sharding import PartitionSpec as P

HD = 128


EPS = 1e-06


def normalize(matrix, gain):
    widened = matrix.astype(jnp.float32)
    inverse = lax.rsqrt(jnp.mean(widened * widened, axis=-1, keepdims=True) + EPS)
    return (widened * inverse * gain).astype(jnp.bfloat16)


def body(queries, keys, values, q_gain, k_gain):
    q_normed = normalize(queries, q_gain)
    k_normed = normalize(keys, k_gain)
    q_local, k_local, v_local = (
        lax.all_to_all(q_normed, "head", split_axis=1, concat_axis=0, tiled=True),
        lax.all_to_all(k_normed, "head", split_axis=1, concat_axis=0, tiled=True),
        lax.all_to_all(values, "head", split_axis=1, concat_axis=0, tiled=True),
    )
    query_count = q_local.shape[0]
    local_heads = q_local.shape[1] // HD
    factor = 1.0 / math.sqrt(HD)
    q_heads = q_local.reshape(query_count, local_heads, HD).transpose(1, 0, 2)
    initial = (
        jnp.full((local_heads, query_count), -1e30, jnp.float32),
        jnp.zeros((local_heads, query_count), jnp.float32),
        jnp.zeros((local_heads, query_count, HD), jnp.float32),
    )
    half_rows = q_local.shape[0]
    key_piece = lax.all_gather(k_local, ("seq", "sub"), axis=0, tiled=True)
    value_piece = lax.all_gather(v_local, ("seq", "sub"), axis=0, tiled=True)
    row_count = key_piece.shape[0]
    block_size = math.gcd(row_count, 512)
    turn_count = row_count // block_size
    key_blocks = key_piece.reshape(turn_count, block_size, local_heads, HD)
    value_blocks = value_piece.reshape(turn_count, block_size, local_heads, HD)

    def advance(state, block_pair):
        key_block, value_block = block_pair
        highest, weight_sum, weighted = state
        scores = (
            jnp.einsum("hqd,khd->hqk", q_heads, key_block, preferred_element_type=jnp.float32)
            * factor
        )
        new_high = jnp.maximum(highest, jnp.max(scores, axis=-1))
        shrink = jnp.exp(highest - new_high)
        weights = jnp.exp(scores - new_high[..., None])
        new_sum = weight_sum * shrink + jnp.sum(weights, axis=-1)
        probs = weights.astype(jnp.bfloat16)
        added = jnp.einsum("hqk,khd->hqd", probs, value_block, preferred_element_type=jnp.float32)
        return ((new_high, new_sum, weighted * shrink[..., None] + added), None)

    partial_value = lax.scan(advance, initial, (key_blocks, value_blocks))[0]
    weight_sum = partial_value[1]
    weighted = partial_value[2]
    result = weighted / weight_sum[..., None]
    outputs = result.transpose(1, 0, 2).reshape(half_rows, local_heads * HD).astype(jnp.bfloat16)
    return lax.all_to_all(outputs, "head", split_axis=0, concat_axis=1, tiled=True)


def solution(mesh):
    in_specs = (
        P(("grp", "seq", "head", "sub"), None),
        P(("grp", "seq", "head", "sub"), None),
        P(("grp", "seq", "head", "sub"), None),
        P(),
        P(),
    )
    out_specs = P(("grp", "seq", "head", "sub"), None)
    return jax.shard_map(body, mesh=mesh, in_specs=in_specs, out_specs=out_specs, check_vma=False)
```

profile of v0, /device:TPU:0, one launch (start us, length us, event | category | flops | bytes accessed | tf_op | source)
XLA Modules:
  0.0 108.0 jit_solution(10044975855559807415)
XLA Ops:
  6.5 0.0 copy-start.1
  6.5 0.0 copy-start
  6.5 0.0 copy-start.2
  6.5 0.0 all-gather.3.cloned.1.call-start
  6.5 1.2 %fusion.12 = f32[24]{0:T(128)S(1)} fusion(bf16[24,5120]{1,0:T(8,128)(2,1)} %param.8), kind=kLoop, calls=%fused_computation.22 | loop fusion | flops 368616 | bytes 245856 | tf_op jit(solution)/shard_map/reduce_sum | solution.py:16
  7.7 1.1 %fusion.14 = bf16[24,5120]{1,0:T(8,128)(2,1)S(1)} fusion(bf16[24,5120]{1,0:T(8,128)(2,1)} %param.8, f32[5120]{0:T(1024)} %param.11, f32[24]{0:T(128)S(1)} %add_rsqrt_fusion.1), kind=kLoop, calls=%fused_computation.24 | loop fusion | flops 491520 | bytes 512096 | tf_op jit(solution)/shard_map/convert_element_type | solution.py:17
  8.8 9.6 %all_to_all.70 = bf16[24,2,2560]{2,0,1:T(8,128)(2,1)} all-to-all(bf16[24,2,2560]{2,0,1:T(8,128)(2,1)S(1)} %bitcast.48), channel_id=1, replica_groups=mesh['grp'=2,'seq'=4,'head'=2,'sub'=2] {'head'}, dimensions={1} | all-to-all | bytes 491520 | tf_op jit(solution)/shard_map/all_to_all | solution.py:25
  18.4 0.0 all-gather.3.cloned.1.call-update
  18.4 0.0 all-gather.5.cloned.1.call-start
  18.5 0.0 copy-done.1
  18.5 8.2 %all_to_all.71 = bf16[24,2,2560]{2,0,1:T(8,128)(2,1)} all-to-all(bf16[24,2,2560]{2,0,1:T(8,128)(2,1)S(1)} %bitcast.50), channel_id=1, replica_groups=mesh['grp'=2,'seq'=4,'head'=2,'sub'=2] {'head'}, dimensions={1} | all-to-all | bytes 491520 | tf_op jit(solution)/shard_map/all_to_all | solution.py:26
  26.7 0.0 all-gather.5.cloned.1.call-update
  26.7 0.0 copy-done
  26.7 0.2 fusion.15
  26.9 0.0 copy-done.2
  26.9 0.1 fusion.17
  27.0 0.7 copy.35
  27.7 3.4 %all-to-all-start.1 = ((bf16[24,2,2560]{2,0,1:T(8,128)(2,1)}), bf16[24,2,2560]{2,0,1:T(8,128)(2,1)S(1)}, u32[]{:S(2)}, u32[]{:S(2)}) async-start(bf16[24,2,2560]{2,0,1:T(8,128)(2,1)} %bitcast.34), calls=%async_computation.1 | async-start | bytes 491520 | tf_op jit(solution)/shard_map/all_to_all | solution.py:24
  31.2 5.0 %all-to-all-done.1 = bf16[24,2,2560]{2,0,1:T(8,128)(2,1)S(1)} async-done(((bf16[24,2,2560]{2,0,1:T(8,128)(2,1)}), bf16[24,2,2560]{2,0,1:T(8,128)(2,1)S(1)}, u32[]{:S(2)}, u32[]{:S(2)}) %all-to-all-start.1) | async-done | bytes 245792 | tf_op jit(solution)/shard_map/all_to_all | solution.py:24
  36.3 0.2 reshape.47
  36.5 10.7 %all-gather.3.cloned.1.call-done = bf16[384,2560]{1,0:T(8,128)(2,1)} async-done(((bf16[48,2560]{1,0:T(8,128)(2,1)}), bf16[384,2560]{1,0:T(8,128)(2,1)}) %all-gather.3.cloned.1.call-update) | async-done | bytes 1966096 | tf_op jit(solution)/shard_map/all_gather | solution.py:38
  47.2 4.3 %reshape.46 = bf16[3,128,20,128]{3,2,1,0:T(8,128)(2,1)} reshape(bf16[384,2560]{1,0:T(8,128)(2,1)} %all-gather.3.cloned.1.call-done) | data formatting | bytes 3932160 | tf_op jit(solution)/shard_map/reshape | solution.py:43
  51.5 2.1 %copy.22 = bf16[3,128,20,128]{3,1,2,0:T(8,128)(2,1)S(1)} copy(bf16[3,128,20,128]{3,2,1,0:T(8,128)(2,1)} %reshape.46) | data formatting | bytes 3932160
  53.7 22.7 %all-gather.5.cloned.1.call-done = bf16[384,2560]{1,0:T(8,128)(2,1)} async-done(((bf16[48,2560]{1,0:T(8,128)(2,1)}), bf16[384,2560]{1,0:T(8,128)(2,1)}) %all-gather.5.cloned.1.call-update) | async-done | bytes 1966096 | tf_op jit(solution)/shard_map/all_gather | solution.py:39
  76.4 4.3 %reshape.48 = bf16[3,128,20,128]{3,2,1,0:T(8,128)(2,1)} reshape(bf16[384,2560]{1,0:T(8,128)(2,1)} %all-gather.5.cloned.1.call-done) | data formatting | bytes 3932160 | tf_op jit(solution)/shard_map/reshape | solution.py:44
  80.7 3.4 %copy.24 = bf16[3,128,20,128]{3,1,2,0:T(8,128)(2,1)} copy(bf16[3,128,20,128]{3,2,1,0:T(8,128)(2,1)} %reshape.48) | data formatting | bytes 3932160
  84.1 7.8 %while.15 = (s32[]{:T(128)}, f32[20,48]{1,0:T(8,128)S(1)}, f32[20,48]{1,0:T(8,128)S(1)}, f32[20,48,128]{2,1,0:T(8,128)S(1)}, bf16[3,128,20,128]{3,1,2,0:T(8,128)...) while((s32[]{:T(128)}, f32[20,48]{1,0:T(8,128)S(1)}, ...), condition=%wide.region_5.6_spmd.clone, body=%wide.region_2.5_spmd.clone.sunk | while | flops 64025280 | bytes 4076141 | solution.py:61
  84.1 0.6 fusion.30
  84.8 0.4 fusion.31
  85.2 1.5 %convolution_add_fusion.2 = f32[20,48,128]{2,1,0:T(8,128)S(1)} fusion(bf16[3,128,20,128]{3,1,2,0:T(8,128)(2,1)} %get-tuple-element.183, s32[]{:T(128)} %get-tuple-element.168, f32[20,48,128]{2,1,0:T(8,128)S(1)} %get-tuple-element.171, f32[20,48,128]{2,1,0:T(8,128)S(1)} %get-tuple-element.156, f32[20,48]{1,0:T(8,128)S(1)} %get-tuple-element.158, ...), kind=kOutput, calls=%fused_computation.clone.1 | convolution fusion | flops 32071680 | bytes 2138113 | tf_op jit(solution)/shard_map/while/body/eval_jaxpr/hqk,khd->hqd/dot_general | solution.py:58
  86.7 0.6 fusion.30
  87.4 0.4 fusion.31
  87.8 1.5 %convolution_add_fusion.2 = f32[20,48,128]{2,1,0:T(8,128)S(1)} fusion(bf16[3,128,20,128]{3,1,2,0:T(8,128)(2,1)} %get-tuple-element.183, s32[]{:T(128)} %get-tuple-element.168, f32[20,48,128]{2,1,0:T(8,128)S(1)} %get-tuple-element.171, f32[20,48,128]{2,1,0:T(8,128)S(1)} %get-tuple-element.156, f32[20,48]{1,0:T(8,128)S(1)} %get-tuple-element.158, ...), kind=kOutput, calls=%fused_computation.clone.1 | convolution fusion | flops 32071680 | bytes 2138113 | tf_op jit(solution)/shard_map/while/body/eval_jaxpr/hqk,khd->hqd/dot_general | solution.py:58
  89.3 0.6 fusion.30
  90.0 0.4 fusion.31
  90.4 1.5 %convolution_add_fusion.2 = f32[20,48,128]{2,1,0:T(8,128)S(1)} fusion(bf16[3,128,20,128]{3,1,2,0:T(8,128)(2,1)} %get-tuple-element.183, s32[]{:T(128)} %get-tuple-element.168, f32[20,48,128]{2,1,0:T(8,128)S(1)} %get-tuple-element.171, f32[20,48,128]{2,1,0:T(8,128)S(1)} %get-tuple-element.156, f32[20,48]{1,0:T(8,128)S(1)} %get-tuple-element.158, ...), kind=kOutput, calls=%fused_computation.clone.1 | convolution fusion | flops 32071680 | bytes 2138113 | tf_op jit(solution)/shard_map/while/body/eval_jaxpr/hqk,khd->hqd/dot_general | solution.py:58
  91.9 0.2 fusion.18
  92.1 0.1 copy.25
  92.2 0.2 convert_element_type.31
  92.4 8.0 %all_to_all.72 = bf16[2,24,2560]{2,1,0:T(8,128)(2,1)S(1)} all-to-all(bf16[2,24,2560]{2,1,0:T(8,128)(2,1)S(1)} %convert_element_type.31), channel_id=1, replica_groups=mesh['grp'=2,'seq'=4,'head'=2,'sub'=2] {'head'}, dimensions={0} | all-to-all | bytes 491520 | tf_op jit(solution)/shard_map/all_to_all | solution.py:66
  100.4 0.7 copy.30
  (17 shorter events, 0.2 us)
Async XLA Ops:
  6.5 11.9 %copy-start.1 = (bf16[24,5120]{1,0:T(8,128)(2,1)S(1)}, bf16[24,5120]{1,0:T(8,128)(2,1)}, u32[]{:S(2)}) copy-start(bf16[24,5120]{1,0:T(8,128)(2,1)} %param.9) | copy-start | bytes 737284
  6.5 20.2 %copy-start = (bf16[24,5120]{1,0:T(8,128)(2,1)S(1)}, bf16[24,5120]{1,0:T(8,128)(2,1)}, u32[]{:S(2)}) copy-start(bf16[24,5120]{1,0:T(8,128)(2,1)} %param.7) | copy-start | bytes 737284
  6.5 20.3 %copy-start.2 = (f32[5120]{0:T(1024)S(1)}, f32[5120]{0:T(1024)}, u32[]{:S(2)}) copy-start(f32[5120]{0:T(1024)} %param.10) | copy-start | bytes 61444
  6.5 40.7 %all-gather.3.cloned.1.call-start = ((), (), s32[]{:S(2)}) async-start(), calls=%async_computation.4 | async-start | bytes 2211840 | tf_op jit(solution)/shard_map/all_gather | solution.py:38
  18.4 57.9 %all-gather.5.cloned.1.call-start = ((), (), s32[]{:S(2)}) async-start(), calls=%async_computation.5 | async-start | bytes 2211840 | tf_op jit(solution)/shard_map/all_gather | solution.py:39
  27.7 8.5 %all-to-all-start.1 = ((bf16[24,2,2560]{2,0,1:T(8,128)(2,1)}), bf16[24,2,2560]{2,0,1:T(8,128)(2,1)S(1)}, u32[]{:S(2)}, u32[]{:S(2)}) async-start(bf16[24,2,2560]{2,0,1:T(8,128)(2,1)} %bitcast.34), calls=%async_computation.1 | async-start | bytes 491520 | tf_op jit(solution)/shard_map/all_to_all | solution.py:24
Sparse Core Ops, SparseCore 0:
  18.5 28.6 all-gather.2
  48.8 27.4 all-gather.4
where the time goes:
time: 109 us; the launch traced here: 108 us
  waiting for transfers between devices  38.5 us (35%)
  blocking collectives  25.8 us (24%)
  local copies, waits for them, and re-layouts  16.2 us (15%)
  between operations  13.5 us (12%)
  matrix products  6.39 us (6%)
  other arithmetic  3.95 us (4%)
  starting transfers between devices  3.48 us (3%)
    all_gather x1, waiting for transfers between devices, body(): value_piece = lax.all_gather(v_local, ('seq', 'sub'), axis=0, tiled=True)  22.7 us
    all_gather x1, waiting for transfers between devices, body(): key_piece = lax.all_gather(k_local, ('seq', 'sub'), axis=0, tiled=True)  10.7 us
    all_to_all x1, blocking collectives, body(): lax.all_to_all(k_normed, 'head', split_axis=1, concat_axis=0, tiled=True)  9.57 us
    all_to_all x1, blocking collectives, body(): lax.all_to_all(values, 'head', split_axis=1, concat_axis=0, tiled=True)  8.16 us
    all_to_all x1, blocking collectives, body(): lax.all_to_all(outputs, 'head', split_axis=0, concat_axis=1, tiled=True)  8.04 us
    unnamed x9, local copies, waits for them, and re-layouts  5.64 us
    all_to_all x1, waiting for transfers between devices, body(): lax.all_to_all(q_normed, 'head', split_axis=1, concat_axis=0, tiled=True)  5.04 us
    dot_general x3, matrix products, advance(): jnp.einsum('hqk,khd->hqd', probs, value_block, preferred_element_type=jnp...  4.47 us
  transfers between devices with their start and end apart: 3, of which 3 were waited for; matrix products, arithmetic and copies ran while one was open for 7% of the time, Pallas kernels for 0%

commit v1 on v0

--- a/solution.py
+++ b/solution.py
@@ -1,8 +1,11 @@
+import functools
 import math
 
 import jax
 import jax.numpy as jnp
 from jax import lax
+from jax.experimental import pallas as pl
+from jax.experimental.pallas import tpu as pltpu
 from jax.sharding import PartitionSpec as P
 
 HD = 128
@@ -66,13 +69,191 @@
     return lax.all_to_all(outputs, "head", split_axis=0, concat_axis=1, tiled=True)
 
 
+MESH = pl.DeviceIdType.MESH
+
+
+def kernel(sizes, rows, heads, q_hbm, k_hbm, v_hbm, qg_ref, kg_ref, out_ref,
+           q_raw, k_raw, q_own, k_own, q_all, k_all, v_all, o_own,
+           load_sem, local_sem, k_send, k_recv, v_send, v_recv, q_send, q_recv, o_send, o_recv):
+    nz, nx, nc = sizes
+    depth = nz // 2
+    groups = depth * nx * nc
+    count = heads // groups
+    width = count * HD
+    z, x, c = lax.axis_index("seq"), lax.axis_index("head"), lax.axis_index("sub")
+    half, place = z // depth, z % depth
+    mine = (place * nx + x) * nc + c
+
+    def peer(dh, dp, dx, dc):
+        tp, tx, tc = lax.rem(place + dp, depth), lax.rem(x + dx, nx), lax.rem(c + dc, nc)
+        tz = lax.rem(half + dh, 2) * depth + tp
+        return {"seq": tz, "head": tx, "sub": tc}, (tp * nx + tx) * nc + tc
+
+    def back(dp, dx, dc):
+        return peer(0, (depth - dp) % depth, (nx - dx) % nx, (nc - dc) % nc)[0]
+
+    near = [(0, dp, dx, dc) for dp in range(depth) for dx in range(nx) for dc in range(nc)]
+    far = [(1, dp, dx, dc) for dp in range(depth) for dx in range(nx) for dc in range(nc)]
+    offsets = near + far
+
+    loads = [
+        pltpu.make_async_copy(q_hbm, q_raw, load_sem.at[0]),
+        pltpu.make_async_copy(k_hbm, k_raw, load_sem.at[1]),
+    ]
+    for load in loads:
+        load.start()
+
+    barrier = pltpu.get_barrier_semaphore()
+    for r in offsets[1:]:
+        pl.semaphore_signal(barrier, inc=1, device_id=peer(*r)[0], device_id_type=MESH)
+
+    def columns(group):
+        return pl.ds(pl.multiple_of(group * width, HD), width)
+
+    local_v = pltpu.make_async_copy(v_hbm.at[:, columns(mine)], v_all.at[0], local_sem.at[0])
+    local_v.start()
+
+    def norm(raw, gain, own):
+        total = jnp.zeros((rows, HD), jnp.float32)
+        for h in range(heads):
+            block = raw[:, h * HD:(h + 1) * HD].astype(jnp.float32)
+            total += block * block
+        mean = jnp.sum(total, axis=-1, keepdims=True) / (heads * HD)
+        inverse = lax.rsqrt(mean + EPS)
+        for h in range(heads):
+            block = raw[:, h * HD:(h + 1) * HD].astype(jnp.float32)
+            j = h % count
+            own[h // count, :, j * HD:(j + 1) * HD] = (
+                block * inverse * gain[h:h + 1, :]
+            ).astype(jnp.bfloat16)
+
+    loads[1].wait()
+    norm(k_raw, kg_ref, k_own)
+    loads[0].wait()
+    norm(q_raw, qg_ref, q_own)
+    pl.semaphore_wait(barrier, len(offsets) - 1)
+
+    order = far + near[1:]
+    v_copies, k_copies, q_copies = {}, {}, {}
+    for r in order:
+        i = offsets.index(r)
+        device, group = peer(*r)
+        v_copies[i] = pltpu.make_async_remote_copy(
+            v_hbm.at[:, columns(group)], v_all.at[i], v_send.at[i], v_recv.at[i],
+            device_id=device, device_id_type=MESH)
+        k_copies[i] = pltpu.make_async_remote_copy(
+            k_own.at[group], k_all.at[i], k_send.at[i], k_recv.at[i],
+            device_id=device, device_id_type=MESH)
+        if r[0] == 0:
+            q_copies[i] = pltpu.make_async_remote_copy(
+                q_own.at[group], q_all.at[i], q_send.at[i], q_recv.at[i],
+                device_id=device, device_id_type=MESH)
+    for pair in zip(far, near):
+        for r in pair:
+            i = offsets.index(r)
+            if i:
+                k_copies[i].start()
+                if i in q_copies:
+                    q_copies[i].start()
+                v_copies[i].start()
+
+    local_k = pltpu.make_async_copy(k_own.at[mine], k_all.at[0], local_sem.at[1])
+    local_q = pltpu.make_async_copy(q_own.at[mine], q_all.at[0], local_sem.at[2])
+    local_k.start()
+    local_q.start()
+    local_k.wait()
+    local_q.wait()
+    local_v.wait()
+    for copies in (q_copies, k_copies, v_copies):
+        for i in sorted(copies):
+            copies[i].wait_recv()
+
+    factor = 1.0 / math.sqrt(HD)
+
+    def stacked(ref, j):
+        block = ref[:, :, j * HD:(j + 1) * HD].astype(jnp.float32)
+        return block.reshape(ref.shape[0] * rows, HD).astype(jnp.bfloat16)
+
+    for j in range(count):
+        q, k, v = stacked(q_all, j), stacked(k_all, j), stacked(v_all, j)
+        scores = lax.dot_general(
+            q, k, (((1,), (1,)), ((), ())), preferred_element_type=jnp.float32) * factor
+        weights = jnp.exp(scores - jnp.max(scores, axis=-1, keepdims=True))
+        weight_sum = jnp.sum(weights, axis=-1, keepdims=True)
+        weighted = jnp.dot(weights.astype(jnp.bfloat16), v, preferred_element_type=jnp.float32)
+        result = (weighted / weight_sum).reshape(groups, rows, HD).astype(jnp.bfloat16)
+        o_own[:, :, j * HD:(j + 1) * HD] = result
+
+    o_copies = []
+    for i, r in enumerate(near):
+        if i:
+            copy = pltpu.make_async_remote_copy(
+                o_own.at[i], out_ref.at[:, columns(mine)], o_send.at[i], o_recv.at[i],
+                device_id=back(*r[1:]), device_id_type=MESH)
+            copy.start()
+            o_copies.append(copy)
+    local_o = pltpu.make_async_copy(o_own.at[0], out_ref.at[:, columns(mine)], local_sem.at[3])
+    local_o.start()
+    for copies in (k_copies, v_copies, q_copies):
+        for i in sorted(copies):
+            copies[i].wait_send()
+    for copy in o_copies:
+        copy.wait_send()
+    for copy in o_copies:
+        copy.wait_recv()
+    local_o.wait()
+
+
+def fused(sizes, queries, keys, values, q_gain, k_gain):
+    rows, total_width = queries.shape
+    heads = total_width // HD
+    nz, nx, nc = sizes
+    groups = nz // 2 * nx * nc
+    width = heads // groups * HD
+    everyone = groups * 2
+    dma = pltpu.SemaphoreType.DMA
+    half = jnp.bfloat16
+    return pl.pallas_call(
+        functools.partial(kernel, sizes, rows, heads),
+        out_shape=jax.ShapeDtypeStruct((rows, total_width), half),
+        in_specs=[pl.BlockSpec(memory_space=pl.ANY)] * 3
+        + [pl.BlockSpec(memory_space=pltpu.VMEM)] * 2,
+        out_specs=pl.BlockSpec(memory_space=pltpu.VMEM),
+        scratch_shapes=[
+            pltpu.VMEM((rows, total_width), half),
+            pltpu.VMEM((rows, total_width), half),
+            pltpu.VMEM((groups, rows, width), half),
+            pltpu.VMEM((groups, rows, width), half),
+            pltpu.VMEM((groups, rows, width), half),
+            pltpu.VMEM((everyone, rows, width), half),
+            pltpu.VMEM((everyone, rows, width), half),
+            pltpu.VMEM((groups, rows, width), half),
+            dma((2,)),
+            dma((4,)),
+            dma((everyone,)),
+            dma((everyone,)),
+            dma((everyone,)),
+            dma((everyone,)),
+            dma((groups,)),
+            dma((groups,)),
+            dma((groups,)),
+            dma((groups,)),
+        ],
+        compiler_params=pltpu.CompilerParams(collective_id=0, has_side_effects=True),
+    )(queries, keys, values, q_gain.reshape(heads, HD), k_gain.reshape(heads, HD))
+
+
 def solution(mesh):
-    in_specs = (
-        P(("grp", "seq", "head", "sub"), None),
-        P(("grp", "seq", "head", "sub"), None),
-        P(("grp", "seq", "head", "sub"), None),
-        P(),
-        P(),
-    )
-    out_specs = P(("grp", "seq", "head", "sub"), None)
-    return jax.shard_map(body, mesh=mesh, in_specs=in_specs, out_specs=out_specs, check_vma=False)
+    spec = P(("grp", "seq", "head", "sub"), None)
+    sizes = (mesh.shape["seq"], mesh.shape["head"], mesh.shape["sub"])
+
+    def run(queries, keys, values, q_gain, k_gain):
+        heads = queries.shape[1] // HD
+        groups = sizes[0] // 2 * sizes[1] * sizes[2]
+        fits = sizes[0] % 2 == 0 and groups <= 16 and heads % groups == 0
+        if fits and queries.shape[0] % 8 == 0:
+            return fused(sizes, queries, keys, values, q_gain, k_gain)
+        return body(queries, keys, values, q_gain, k_gain)
+
+    return jax.shard_map(
+        run, mesh=mesh, in_specs=(spec, spec, spec, P(), P()), out_specs=spec, check_vma=False)

time: 109 us -> 39.9 us (0.37)
  waiting for transfers between devices: 38.5 us -> 0 us
  Pallas kernels: 0 us -> 38.1 us
  blocking collectives: 25.8 us -> 0 us
  local copies, waits for them, and re-layouts: 16.2 us -> 1.65 us
  between operations: 13.5 us -> 0.01 us
  matrix products: 6.39 us -> 0 us
  other arithmetic: 3.95 us -> 0 us
  starting transfers between devices: 3.48 us -> 0 us
    pallas_call x0 -> x1, Pallas kernels: none -> 38.1 us  [fused(): pl.pallas_call(functools.partial(kernel, sizes, rows, heads), out_shape=j...]
    all_gather x2 -> x0, waiting for transfers between devices: 33.4 us -> none  [the longest x1 22.7 us: body(): value_piece = lax.all_gather(v_local, ('seq', 'sub'), axis=0, tiled=True)]
    all_to_all x3 -> x0, blocking collectives: 25.8 us -> none  [the longest x1 9.57 us: body(): lax.all_to_all(k_normed, 'head', split_axis=1, concat_axis=0, tiled=True)]
    reshape x3 -> x0, local copies, waits for them, and re-layouts: 8.85 us -> none  [the longest x1 4.34 us: body(): key_blocks = key_piece.reshape(turn_count, block_size, local_heads, HD)]
    dot_general x6 -> x0, matrix products: 6.39 us -> none  [the longest x3 4.47 us: advance(): jnp.einsum('hqk,khd->hqd', probs, value_block, preferred_element_type=jnp...]
    all_to_all x1 -> x0, waiting for transfers between devices: 5.04 us -> none  [body(): lax.all_to_all(q_normed, 'head', split_axis=1, concat_axis=0, tiled=True)]
    unnamed x9 -> x1, local copies, waits for them, and re-layouts: 5.64 us -> 1.65 us
    all_to_all x1 -> x0, starting transfers between devices: 3.44 us -> none  [body(): lax.all_to_all(q_normed, 'head', split_axis=1, concat_axis=0, tiled=True)]
  transfers between devices with their start and end apart: 3 -> 0, of which waited for: 3 -> 0; matrix products, arithmetic and copies ran while one was open for 7% -> 0% of each run, Pallas kernels for 0% -> 0%
where the time goes in v1:
time: 39.9 us; the launch traced here: 39.7 us
  Pallas kernels  38.1 us (95%)
  local copies, waits for them, and re-layouts  1.65 us (4%)
    pallas_call x1, Pallas kernels, fused(): pl.pallas_call(functools.partial(kernel, sizes, rows, heads), out_shape=j...  38.1 us
    unnamed x1, local copies, waits for them, and re-layouts  1.65 us

profile of v1, /device:TPU:0, one launch (start us, length us, event | category | flops | bytes accessed | tf_op | source)
XLA Modules:
  0.0 39.7 jit_solution(18390320929346320340)
XLA Ops:
  0.0 38.1 %shard_map.55 = bf16[24,5120]{1,0:T(8,128)(2,1)} custom-call(bf16[24,5120]{1,0:T(8,128)(2,1)} %q_hbm.1, bf16[24,5120]{1,0:T(8,128)(2,1)} %k_hbm.1, bf16[24,5120]{1,0:T(8,128)(2,1)} %v_hbm.1, f32[40,128]{1,0:T(8,128)} %bitcast.2, f32[40,128]{1,0:T(8,128)} %bitcast.3), custom_call_target="tpu_custom_call" | custom-call | tf_op jit(solution)/shard_map/pallas_call | solution.py:216
  38.1 1.7 %copy.7 = bf16[24,5120]{1,0:T(8,128)(2,1)} copy(bf16[24,5120]{1,0:T(8,128)(2,1)} %shard_map.55) | data formatting | bytes 491520

commit v2 on v1

--- a/solution.py
+++ b/solution.py
@@ -70,16 +70,24 @@
 
 
 MESH = pl.DeviceIdType.MESH
-
-
-def kernel(sizes, rows, heads, q_hbm, k_hbm, v_hbm, qg_ref, kg_ref, out_ref,
-           q_raw, k_raw, q_own, k_own, q_all, k_all, v_all, o_own,
-           load_sem, local_sem, k_send, k_recv, v_send, v_recv, q_send, q_recv, o_send, o_recv):
+CHUNK = 2
+AHEAD = 2
+
+
+def spans_of(count):
+    return [(first, min(CHUNK, count - first)) for first in range(0, count, CHUNK)]
+
+
+def kernel(sizes, rows, heads, q_hbm, k_hbm, v_hbm, qg_ref, kg_ref, out_ref, q_raw, k_raw, *rest):
     nz, nx, nc = sizes
     depth = nz // 2
     groups = depth * nx * nc
     count = heads // groups
     width = count * HD
+    spans = spans_of(count)
+    steps = len(spans)
+    own, every, o_own, o_all = (rest[i * steps:(i + 1) * steps] for i in range(4))
+    load_sem, stage_sem, local_sem, send_sem, recv_sem, o_send, o_recv, o_store = rest[4 * steps:]
     z, x, c = lax.axis_index("seq"), lax.axis_index("head"), lax.axis_index("sub")
     half, place = z // depth, z % depth
     mine = (place * nx + x) * nc + c
@@ -107,13 +115,16 @@
     for r in offsets[1:]:
         pl.semaphore_signal(barrier, inc=1, device_id=peer(*r)[0], device_id_type=MESH)
 
-    def columns(group):
-        return pl.ds(pl.multiple_of(group * width, HD), width)
-
-    local_v = pltpu.make_async_copy(v_hbm.at[:, columns(mine)], v_all.at[0], local_sem.at[0])
-    local_v.start()
-
-    def norm(raw, gain, own):
+    stages = []
+    for n, (first, held) in enumerate(spans):
+        for group in range(groups):
+            start = group * width + first * HD
+            stages.append(pltpu.make_async_copy(
+                v_hbm.at[:, start:start + held * HD], own[n].at[group, 1],
+                stage_sem.at[n, group]))
+            stages[-1].start()
+
+    def norm(raw, gain, which):
         total = jnp.zeros((rows, HD), jnp.float32)
         for h in range(heads):
             block = raw[:, h * HD:(h + 1) * HD].astype(jnp.float32)
@@ -122,86 +133,100 @@
         inverse = lax.rsqrt(mean + EPS)
         for h in range(heads):
             block = raw[:, h * HD:(h + 1) * HD].astype(jnp.float32)
-            j = h % count
-            own[h // count, :, j * HD:(j + 1) * HD] = (
+            n, j = h % count // CHUNK, h % count % CHUNK
+            own[n][h // count, which, :, j * HD:(j + 1) * HD] = (
                 block * inverse * gain[h:h + 1, :]
             ).astype(jnp.bfloat16)
 
     loads[1].wait()
-    norm(k_raw, kg_ref, k_own)
+    norm(k_raw, kg_ref, 0)
     loads[0].wait()
-    norm(q_raw, qg_ref, q_own)
+    norm(q_raw, qg_ref, 2)
+    for stage in stages:
+        stage.wait()
     pl.semaphore_wait(barrier, len(offsets) - 1)
 
-    order = far + near[1:]
-    v_copies, k_copies, q_copies = {}, {}, {}
-    for r in order:
-        i = offsets.index(r)
-        device, group = peer(*r)
-        v_copies[i] = pltpu.make_async_remote_copy(
-            v_hbm.at[:, columns(group)], v_all.at[i], v_send.at[i], v_recv.at[i],
-            device_id=device, device_id_type=MESH)
-        k_copies[i] = pltpu.make_async_remote_copy(
-            k_own.at[group], k_all.at[i], k_send.at[i], k_recv.at[i],
-            device_id=device, device_id_type=MESH)
-        if r[0] == 0:
-            q_copies[i] = pltpu.make_async_remote_copy(
-                q_own.at[group], q_all.at[i], q_send.at[i], q_recv.at[i],
-                device_id=device, device_id_type=MESH)
-    for pair in zip(far, near):
-        for r in pair:
+    def copies_of(n):
+        found = []
+        for r in near[1:] + far:
             i = offsets.index(r)
-            if i:
-                k_copies[i].start()
-                if i in q_copies:
-                    q_copies[i].start()
-                v_copies[i].start()
-
-    local_k = pltpu.make_async_copy(k_own.at[mine], k_all.at[0], local_sem.at[1])
-    local_q = pltpu.make_async_copy(q_own.at[mine], q_all.at[0], local_sem.at[2])
-    local_k.start()
-    local_q.start()
-    local_k.wait()
-    local_q.wait()
-    local_v.wait()
-    for copies in (q_copies, k_copies, v_copies):
-        for i in sorted(copies):
-            copies[i].wait_recv()
+            device, group = peer(*r)
+            source, target = own[n].at[group], every[n].at[i]
+            if r[0]:
+                source, target = own[n].at[group, 0:2], every[n].at[i, 0:2]
+            found.append(pltpu.make_async_remote_copy(
+                source, target, send_sem.at[n, i], recv_sem.at[n, i],
+                device_id=device, device_id_type=MESH))
+        return found
+
+    copies = [copies_of(n) for n in range(steps)]
+    locals_ = [
+        pltpu.make_async_copy(own[n].at[mine], every[n].at[0], local_sem.at[n])
+        for n in range(steps)
+    ]
+
+    def send(n):
+        if n < steps:
+            for copy in copies[n]:
+                copy.start()
+            locals_[n].start()
+
+    for n in range(AHEAD):
+        send(n)
 
     factor = 1.0 / math.sqrt(HD)
 
-    def stacked(ref, j):
-        block = ref[:, :, j * HD:(j + 1) * HD].astype(jnp.float32)
-        return block.reshape(ref.shape[0] * rows, HD).astype(jnp.bfloat16)
-
-    for j in range(count):
-        q, k, v = stacked(q_all, j), stacked(k_all, j), stacked(v_all, j)
+    def stacked(ref, slots, which, j):
+        block = ref[0:slots, which, :, j * HD:(j + 1) * HD].astype(jnp.float32)
+        return block.reshape(slots * rows, HD).astype(jnp.bfloat16)
+
+    def attend(n, j):
+        k, v = stacked(every[n], 2 * groups, 0, j), stacked(every[n], 2 * groups, 1, j)
+        q = stacked(every[n], groups, 2, j)
         scores = lax.dot_general(
             q, k, (((1,), (1,)), ((), ())), preferred_element_type=jnp.float32) * factor
         weights = jnp.exp(scores - jnp.max(scores, axis=-1, keepdims=True))
         weight_sum = jnp.sum(weights, axis=-1, keepdims=True)
         weighted = jnp.dot(weights.astype(jnp.bfloat16), v, preferred_element_type=jnp.float32)
         result = (weighted / weight_sum).reshape(groups, rows, HD).astype(jnp.bfloat16)
-        o_own[:, :, j * HD:(j + 1) * HD] = result
-
-    o_copies = []
-    for i, r in enumerate(near):
-        if i:
-            copy = pltpu.make_async_remote_copy(
-                o_own.at[i], out_ref.at[:, columns(mine)], o_send.at[i], o_recv.at[i],
-                device_id=back(*r[1:]), device_id_type=MESH)
+        o_own[n][:, :, j * HD:(j + 1) * HD] = result
+
+    def out_columns(n, group):
+        first, held = spans[n]
+        return out_ref.at[:, pl.ds(pl.multiple_of(group * width + first * HD, HD), held * HD)]
+
+    o_copies, stores = [], []
+    for n, (first, held) in enumerate(spans):
+        locals_[n].wait()
+        for copy in copies[n]:
+            copy.wait_recv()
+        for j in range(held):
+            attend(n, j)
+        for i, r in enumerate(near):
+            if i:
+                copy = pltpu.make_async_remote_copy(
+                    o_own[n].at[i], o_all[n].at[i], o_send.at[n, i], o_recv.at[n, i],
+                    device_id=back(*r[1:]), device_id_type=MESH)
+                o_copies.append((n, i, r, copy))
+            else:
+                copy = pltpu.make_async_copy(
+                    o_own[n].at[i], out_columns(n, mine), o_store.at[n, i])
+                stores.append(copy)
             copy.start()
-            o_copies.append(copy)
-    local_o = pltpu.make_async_copy(o_own.at[0], out_ref.at[:, columns(mine)], local_sem.at[3])
-    local_o.start()
-    for copies in (k_copies, v_copies, q_copies):
-        for i in sorted(copies):
-            copies[i].wait_send()
-    for copy in o_copies:
+        send(n + AHEAD)
+    for n, i, r, copy in o_copies:
+        copy.wait_recv()
+        store = pltpu.make_async_copy(
+            o_all[n].at[i], out_columns(n, peer(*r)[1]), o_store.at[n, i])
+        store.start()
+        stores.append(store)
+    for some in copies:
+        for copy in some:
+            copy.wait_send()
+    for _, _, _, copy in o_copies:
         copy.wait_send()
-    for copy in o_copies:
-        copy.wait_recv()
-    local_o.wait()
+    for copy in stores:
+        copy.wait()
 
 
 def fused(sizes, queries, keys, values, q_gain, k_gain):
@@ -209,8 +234,8 @@
     heads = total_width // HD
     nz, nx, nc = sizes
     groups = nz // 2 * nx * nc
-    width = heads // groups * HD
-    everyone = groups * 2
+    spans = spans_of(heads // groups)
+    steps = len(spans)
     dma = pltpu.SemaphoreType.DMA
     half = jnp.bfloat16
     return pl.pallas_call(
@@ -218,26 +243,22 @@
         out_shape=jax.ShapeDtypeStruct((rows, total_width), half),
         in_specs=[pl.BlockSpec(memory_space=pl.ANY)] * 3
         + [pl.BlockSpec(memory_space=pltpu.VMEM)] * 2,
-        out_specs=pl.BlockSpec(memory_space=pltpu.VMEM),
+        out_specs=pl.BlockSpec(memory_space=pl.ANY),
         scratch_shapes=[
             pltpu.VMEM((rows, total_width), half),
             pltpu.VMEM((rows, total_width), half),
-            pltpu.VMEM((groups, rows, width), half),
-            pltpu.VMEM((groups, rows, width), half),
-            pltpu.VMEM((groups, rows, width), half),
-            pltpu.VMEM((everyone, rows, width), half),
-            pltpu.VMEM((everyone, rows, width), half),
-            pltpu.VMEM((groups, rows, width), half),
+            *[pltpu.VMEM((groups, 3, rows, held * HD), half) for _, held in spans],
+            *[pltpu.VMEM((2 * groups, 3, rows, held * HD), half) for _, held in spans],
+            *[pltpu.VMEM((groups, rows, held * HD), half) for _, held in spans],
+            *[pltpu.VMEM((groups, rows, held * HD), half) for _, held in spans],
             dma((2,)),
-            dma((4,)),
-            dma((everyone,)),
-            dma((everyone,)),
-            dma((everyone,)),
-            dma((everyone,)),
-            dma((groups,)),
-            dma((groups,)),
-            dma((groups,)),
-            dma((groups,)),
+            dma((steps, groups)),
+            dma((steps,)),
+            dma((steps, 2 * groups)),
+            dma((steps, 2 * groups)),
+            dma((steps, groups)),
+            dma((steps, groups)),
+            dma((steps, groups)),
         ],
         compiler_params=pltpu.CompilerParams(collective_id=0, has_side_effects=True),
     )(queries, keys, values, q_gain.reshape(heads, HD), k_gain.reshape(heads, HD))

time: 39.9 us -> 37.2 us (0.932)
  Pallas kernels: 38.1 us -> 35.3 us
    pallas_call x1, Pallas kernels: 38.1 us -> 35.3 us  [fused(): pl.pallas_call(functools.partial(kernel, sizes, rows, heads), out_shape=j...]
where the time goes in v2:
time: 37.2 us; the launch traced here: 37 us
  Pallas kernels  35.3 us (95%)
  local copies, waits for them, and re-layouts  1.65 us (4%)
    pallas_call x1, Pallas kernels, fused(): pl.pallas_call(functools.partial(kernel, sizes, rows, heads), out_shape=j...  35.3 us
    unnamed x1, local copies, waits for them, and re-layouts  1.65 us

profile of v2, /device:TPU:0, one launch (start us, length us, event | category | flops | bytes accessed | tf_op | source)
XLA Modules:
  0.0 37.0 jit_solution(721832983857861454)
XLA Ops:
  0.0 35.3 %shard_map.55 = bf16[24,5120]{1,0:T(8,128)(2,1)} custom-call(bf16[24,5120]{1,0:T(8,128)(2,1)} %q_hbm.1, bf16[24,5120]{1,0:T(8,128)(2,1)} %k_hbm.1, bf16[24,5120]{1,0:T(8,128)(2,1)} %v_hbm.1, f32[40,128]{1,0:T(8,128)} %bitcast.2, f32[40,128]{1,0:T(8,128)} %bitcast.3), custom_call_target="tpu_custom_call" | custom-call | tf_op jit(solution)/shard_map/pallas_call | solution.py:241
  35.3 1.7 %copy.7 = bf16[24,5120]{1,0:T(8,128)(2,1)} copy(bf16[24,5120]{1,0:T(8,128)(2,1)} %shard_map.55) | data formatting | bytes 491520

commit v3 on v2

--- a/solution.py
+++ b/solution.py
@@ -70,15 +70,21 @@
 
 
 MESH = pl.DeviceIdType.MESH
-CHUNK = 2
-AHEAD = 2
+SPANS = (4, 1)
 
 
 def spans_of(count):
-    return [(first, min(CHUNK, count - first)) for first in range(0, count, CHUNK)]
-
-
-def kernel(sizes, rows, heads, q_hbm, k_hbm, v_hbm, qg_ref, kg_ref, out_ref, q_raw, k_raw, *rest):
+    found, first = [], 0
+    for held in SPANS:
+        if first < count:
+            found.append((first, min(held, count - first)))
+            first += held
+    if first < count:
+        found.append((first, count - first))
+    return found
+
+
+def kernel(sizes, rows, heads, q_hbm, k_hbm, v_hbm, qg_ref, kg_ref, out_ref, q_raw, k_raw, v_raw, own, every, *rest):
     nz, nx, nc = sizes
     depth = nz // 2
     groups = depth * nx * nc
@@ -86,8 +92,9 @@
     width = count * HD
     spans = spans_of(count)
     steps = len(spans)
-    own, every, o_own, o_all = (rest[i * steps:(i + 1) * steps] for i in range(4))
-    load_sem, stage_sem, local_sem, send_sem, recv_sem, o_send, o_recv, o_store = rest[4 * steps:]
+    o_own, o_all = rest[:steps], rest[steps:2 * steps]
+    (load_sem, local_sem, near_send, near_recv, far_send, far_recv,
+     o_send, o_recv, o_store) = rest[2 * steps:]
     z, x, c = lax.axis_index("seq"), lax.axis_index("head"), lax.axis_index("sub")
     half, place = z // depth, z % depth
     mine = (place * nx + x) * nc + c
@@ -107,6 +114,7 @@
     loads = [
         pltpu.make_async_copy(q_hbm, q_raw, load_sem.at[0]),
         pltpu.make_async_copy(k_hbm, k_raw, load_sem.at[1]),
+        pltpu.make_async_copy(v_hbm, v_raw, load_sem.at[2]),
     ]
     for load in loads:
         load.start()
@@ -115,16 +123,7 @@
     for r in offsets[1:]:
         pl.semaphore_signal(barrier, inc=1, device_id=peer(*r)[0], device_id_type=MESH)
 
-    stages = []
-    for n, (first, held) in enumerate(spans):
-        for group in range(groups):
-            start = group * width + first * HD
-            stages.append(pltpu.make_async_copy(
-                v_hbm.at[:, start:start + held * HD], own[n].at[group, 1],
-                stage_sem.at[n, group]))
-            stages[-1].start()
-
-    def norm(raw, gain, which):
+    def norm(raw, gain, place_of):
         total = jnp.zeros((rows, HD), jnp.float32)
         for h in range(heads):
             block = raw[:, h * HD:(h + 1) * HD].astype(jnp.float32)
@@ -133,56 +132,51 @@
         inverse = lax.rsqrt(mean + EPS)
         for h in range(heads):
             block = raw[:, h * HD:(h + 1) * HD].astype(jnp.float32)
-            n, j = h % count // CHUNK, h % count % CHUNK
-            own[n][h // count, which, :, j * HD:(j + 1) * HD] = (
+            own[h // count, place_of(h % count)] = (
                 block * inverse * gain[h:h + 1, :]
             ).astype(jnp.bfloat16)
 
     loads[1].wait()
-    norm(k_raw, kg_ref, 0)
+    norm(k_raw, kg_ref, lambda j: 2 * j)
     loads[0].wait()
-    norm(q_raw, qg_ref, 2)
-    for stage in stages:
-        stage.wait()
+    norm(q_raw, qg_ref, lambda j: 2 * count + j)
+    loads[2].wait()
+    for h in range(heads):
+        own[h // count, 2 * (h % count) + 1] = v_raw[:, h * HD:(h + 1) * HD]
     pl.semaphore_wait(barrier, len(offsets) - 1)
 
-    def copies_of(n):
-        found = []
-        for r in near[1:] + far:
-            i = offsets.index(r)
-            device, group = peer(*r)
-            source, target = own[n].at[group], every[n].at[i]
-            if r[0]:
-                source, target = own[n].at[group, 0:2], every[n].at[i, 0:2]
-            found.append(pltpu.make_async_remote_copy(
-                source, target, send_sem.at[n, i], recv_sem.at[n, i],
+    near_copies, far_copies = [], [[] for _ in spans]
+    for i, r in enumerate(offsets):
+        device, group = peer(*r)
+        if r[0]:
+            for n, (first, held) in enumerate(spans):
+                part = slice(2 * first, 2 * (first + held))
+                far_copies[n].append(pltpu.make_async_remote_copy(
+                    own.at[group, part], every.at[i, part],
+                    far_send.at[n, i - groups], far_recv.at[n, i - groups],
+                    device_id=device, device_id_type=MESH))
+        elif i:
+            near_copies.append(pltpu.make_async_remote_copy(
+                own.at[group], every.at[i], near_send.at[i], near_recv.at[i],
                 device_id=device, device_id_type=MESH))
-        return found
-
-    copies = [copies_of(n) for n in range(steps)]
-    locals_ = [
-        pltpu.make_async_copy(own[n].at[mine], every[n].at[0], local_sem.at[n])
-        for n in range(steps)
-    ]
-
-    def send(n):
-        if n < steps:
-            for copy in copies[n]:
-                copy.start()
-            locals_[n].start()
-
-    for n in range(AHEAD):
-        send(n)
+    for copy in near_copies:
+        copy.start()
+    for some in far_copies:
+        for copy in some:
+            copy.start()
+    local = pltpu.make_async_copy(own.at[mine], every.at[0], local_sem)
+    local.start()
+    local.wait()
 
     factor = 1.0 / math.sqrt(HD)
 
-    def stacked(ref, slots, which, j):
-        block = ref[0:slots, which, :, j * HD:(j + 1) * HD].astype(jnp.float32)
+    def stacked(slots, index):
+        block = every[0:slots, index].astype(jnp.float32)
         return block.reshape(slots * rows, HD).astype(jnp.bfloat16)
 
-    def attend(n, j):
-        k, v = stacked(every[n], 2 * groups, 0, j), stacked(every[n], 2 * groups, 1, j)
-        q = stacked(every[n], groups, 2, j)
+    def attend(n, first, j):
+        k, v = stacked(2 * groups, 2 * (first + j)), stacked(2 * groups, 2 * (first + j) + 1)
+        q = stacked(groups, 2 * count + first + j)
         scores = lax.dot_general(
             q, k, (((1,), (1,)), ((), ())), preferred_element_type=jnp.float32) * factor
         weights = jnp.exp(scores - jnp.max(scores, axis=-1, keepdims=True))
@@ -197,11 +191,13 @@
 
     o_copies, stores = [], []
     for n, (first, held) in enumerate(spans):
-        locals_[n].wait()
-        for copy in copies[n]:
+        if n == 0:
+            for copy in near_copies:
+                copy.wait_recv()
+        for copy in far_copies[n]:
             copy.wait_recv()
         for j in range(held):
-            attend(n, j)
+            attend(n, first, j)
         for i, r in enumerate(near):
             if i:
                 copy = pltpu.make_async_remote_copy(
@@ -213,14 +209,13 @@
                     o_own[n].at[i], out_columns(n, mine), o_store.at[n, i])
                 stores.append(copy)
             copy.start()
-        send(n + AHEAD)
     for n, i, r, copy in o_copies:
         copy.wait_recv()
         store = pltpu.make_async_copy(
             o_all[n].at[i], out_columns(n, peer(*r)[1]), o_store.at[n, i])
         store.start()
         stores.append(store)
-    for some in copies:
+    for some in [near_copies] + far_copies:
         for copy in some:
             copy.wait_send()
     for _, _, _, copy in o_copies:
@@ -234,7 +229,8 @@
     heads = total_width // HD
     nz, nx, nc = sizes
     groups = nz // 2 * nx * nc
-    spans = spans_of(heads // groups)
+    count = heads // groups
+    spans = spans_of(count)
     steps = len(spans)
     dma = pltpu.SemaphoreType.DMA
     half = jnp.bfloat16
@@ -247,15 +243,17 @@
         scratch_shapes=[
             pltpu.VMEM((rows, total_width), half),
             pltpu.VMEM((rows, total_width), half),
-            *[pltpu.VMEM((groups, 3, rows, held * HD), half) for _, held in spans],
-            *[pltpu.VMEM((2 * groups, 3, rows, held * HD), half) for _, held in spans],
+            pltpu.VMEM((rows, total_width), half),
+            pltpu.VMEM((groups, 3 * count, rows, HD), half),
+            pltpu.VMEM((2 * groups, 3 * count, rows, HD), half),
             *[pltpu.VMEM((groups, rows, held * HD), half) for _, held in spans],
             *[pltpu.VMEM((groups, rows, held * HD), half) for _, held in spans],
-            dma((2,)),
-            dma((steps, groups)),
-            dma((steps,)),
-            dma((steps, 2 * groups)),
-            dma((steps, 2 * groups)),
+            dma((3,)),
+            dma(()),
+            dma((groups,)),
+            dma((groups,)),
+            dma((steps, groups)),
+            dma((steps, groups)),
             dma((steps, groups)),
             dma((steps, groups)),
             dma((steps, groups)),

time: 37.2 us -> 36.5 us (0.981)
  Pallas kernels: 35.3 us -> 34.6 us
    pallas_call x1, Pallas kernels: 35.3 us -> 34.6 us  [fused(): pl.pallas_call(functools.partial(kernel, sizes, rows, heads), out_shape=j...]
where the time goes in v3:
time: 36.5 us; the launch traced here: 36.3 us
  Pallas kernels  34.6 us (95%)
  local copies, waits for them, and re-layouts  1.65 us (5%)
    pallas_call x1, Pallas kernels, fused(): pl.pallas_call(functools.partial(kernel, sizes, rows, heads), out_shape=j...  34.6 us
    unnamed x1, local copies, waits for them, and re-layouts  1.65 us

profile of v3, /device:TPU:0, one launch (start us, length us, event | category | flops | bytes accessed | tf_op | source)
XLA Modules:
  0.0 36.3 jit_solution(15997123917782215771)
XLA Ops:
  0.0 34.6 %shard_map.55 = bf16[24,5120]{1,0:T(8,128)(2,1)} custom-call(bf16[24,5120]{1,0:T(8,128)(2,1)} %q_hbm.1, bf16[24,5120]{1,0:T(8,128)(2,1)} %k_hbm.1, bf16[24,5120]{1,0:T(8,128)(2,1)} %v_hbm.1, f32[40,128]{1,0:T(8,128)} %bitcast.2, f32[40,128]{1,0:T(8,128)} %bitcast.3), custom_call_target="tpu_custom_call" | custom-call | tf_op jit(solution)/shard_map/pallas_call | solution.py:237
  34.6 1.7 %copy.7 = bf16[24,5120]{1,0:T(8,128)(2,1)} copy(bf16[24,5120]{1,0:T(8,128)(2,1)} %shard_map.55) | data formatting | bytes 491520

commit v4 on v3

--- a/solution.py
+++ b/solution.py
@@ -108,7 +108,7 @@
         return peer(0, (depth - dp) % depth, (nx - dx) % nx, (nc - dc) % nc)[0]
 
     near = [(0, dp, dx, dc) for dp in range(depth) for dx in range(nx) for dc in range(nc)]
-    far = [(1, dp, dx, dc) for dp in range(depth) for dx in range(nx) for dc in range(nc)]
+    far = [(1, dp, dx, dc) for dx in range(nx) for dc in range(nc) for dp in reversed(range(depth))]
     offsets = near + far
 
     loads = [
@@ -201,7 +201,7 @@
         for i, r in enumerate(near):
             if i:
                 copy = pltpu.make_async_remote_copy(
-                    o_own[n].at[i], o_all[n].at[i], o_send.at[n, i], o_recv.at[n, i],
+                    o_own[n].at[i], out_columns(n, mine), o_send.at[n, i], o_recv.at[n, i],
                     device_id=back(*r[1:]), device_id_type=MESH)
                 o_copies.append((n, i, r, copy))
             else:
@@ -211,10 +211,6 @@
             copy.start()
     for n, i, r, copy in o_copies:
         copy.wait_recv()
-        store = pltpu.make_async_copy(
-            o_all[n].at[i], out_columns(n, peer(*r)[1]), o_store.at[n, i])
-        store.start()
-        stores.append(store)
     for some in [near_copies] + far_copies:
         for copy in some:
             copy.wait_send()

time: 36.5 us -> 35.7 us (0.978)
  Pallas kernels: 34.6 us -> 33.8 us
    pallas_call x1, Pallas kernels: 34.6 us -> 33.8 us  [fused(): pl.pallas_call(functools.partial(kernel, sizes, rows, heads), out_shape=j...]
where the time goes in v4:
time: 35.7 us; the launch traced here: 35.5 us
  Pallas kernels  33.8 us (95%)
  local copies, waits for them, and re-layouts  1.65 us (5%)
    pallas_call x1, Pallas kernels, fused(): pl.pallas_call(functools.partial(kernel, sizes, rows, heads), out_shape=j...  33.8 us
    unnamed x1, local copies, waits for them, and re-layouts  1.65 us

profile of v4, /device:TPU:0, one launch (start us, length us, event | category | flops | bytes accessed | tf_op | source)
XLA Modules:
  0.0 35.5 jit_solution(14179666376872030225)
XLA Ops:
  0.0 33.8 %shard_map.55 = bf16[24,5120]{1,0:T(8,128)(2,1)} custom-call(bf16[24,5120]{1,0:T(8,128)(2,1)} %q_hbm.1, bf16[24,5120]{1,0:T(8,128)(2,1)} %k_hbm.1, bf16[24,5120]{1,0:T(8,128)(2,1)} %v_hbm.1, f32[40,128]{1,0:T(8,128)} %bitcast.2, f32[40,128]{1,0:T(8,128)} %bitcast.3), custom_call_target="tpu_custom_call" | custom-call | tf_op jit(solution)/shard_map/pallas_call | solution.py:233
  33.8 1.7 %copy.7 = bf16[24,5120]{1,0:T(8,128)(2,1)} copy(bf16[24,5120]{1,0:T(8,128)(2,1)} %shard_map.55) | data formatting | bytes 491520
